TPU v7x, 32 devices: a whole 2x2x4 slice. The times are simulated.
32 devices in a mesh: row: 8 (over y, x, core), col: 4 (over z).
Axes of the slice: x: 2, y: 2, z: 4, core: 2. Of those that a mesh axis runs over, the one named last changes fastest.
Arguments:
- tokens: bfloat16 [32768, 768], P(('row', 'col')), may hold values from -6 to 6
- segment: int32 [32, 1024], replicated, may hold values from 0 to 63, never falling along the last dimension, each value on 1 to 512 neighbouring positions
- w_qkv: bfloat16 [768, 2304], P('row', 'col'), may hold values from -0.21875 to 0.21875
- w_out: bfloat16 [768, 768], P('row', 'col'), may hold values from -0.875 to 0.875
- w_up: bfloat16 [768, 3072], P('row', 'col'), may hold values from -0.21875 to 0.21875
- w_down: bfloat16 [3072, 768], P('row', 'col'), may hold values from -0.109375 to 0.109375
- bias_query: float32 [768], replicated, may hold values from -3 to 3
- bias_value: float32 [768], replicated, may hold values from -3 to 3
- bias_out: float32 [768], replicated, may hold values from -3 to 3
- gain_attn: float32 [768], replicated, may hold values from 0.25 to 1.75
- shift_attn: float32 [768], replicated, may hold values from -3 to 3
- bias_up: float32 [3072], replicated, may hold values from -3 to 3
- bias_down: float32 [768], replicated, may hold values from -3 to 3
- gain_ffn: float32 [768], replicated, may hold values from 0.25 to 1.75
- shift_ffn: float32 [768], replicated, may hold values from -3 to 3
- cotangent: bfloat16 [32768, 768], P(('row', 'col')), may hold values from -6 to 6
Outputs:
- layer_out: bfloat16 [32768, 768], P(('row', 'col'))
- grad_tokens: float32 [32768, 768], P(('row', 'col'))
- grad_qkv: float32 [768, 2304], P('row', 'col')
- grad_out: float32 [768, 768], P('row', 'col')
- grad_up: float32 [768, 3072], P('row', 'col')
- grad_down: float32 [3072, 768], P('row', 'col')
- grad_bias_query: float32 [768], replicated
- grad_bias_value: float32 [768], replicated
- grad_bias_out: float32 [768], replicated
- grad_gain_attn: float32 [768], replicated
- grad_shift_attn: float32 [768], replicated
- grad_bias_up: float32 [3072], replicated
- grad_bias_down: float32 [768], replicated
- grad_gain_ffn: float32 [768], replicated
- grad_shift_ffn: float32 [768], replicated
Inputs may be any that keep to these rules, and one draw needn't show every extreme that they name: `segment`: within each packed sequence the document numbers never fall; a document is a run of equal numbers, and some document has 512 tokens.
All inputs are finite; a program needn't handle non-finite values.
Results may differ from a plain program's by a relative error of at most 0.019.
Values may be sent and summed in bfloat16 or wider, within the bound.
A program may use at most 192 MiB of HBM per device.

v0:
```python
import jax
import jax.numpy as jnp
from jax import lax
from jax.sharding import PartitionSpec as P

HEADS = 12
HEAD_DIM = 64
LEN = 1024
norm_eps = 1e-05
masked_score = -1e30


def gather_block(blocks):
    widened = (
        lax.all_gather(blocks[0], "col", axis=1, tiled=True),
        lax.all_gather(blocks[1], "col", axis=1, tiled=True),
    )
    return (
        lax.all_gather(widened[0], "row", axis=0, tiled=True),
        lax.all_gather(widened[1], "row", axis=0, tiled=True),
    )


def reduce_grads(grads):
    narrowed = (
        lax.psum_scatter(
            grads[0].astype(jnp.bfloat16), "col", scatter_dimension=1, tiled=True
        ).astype(jnp.float32),
        lax.psum_scatter(
            grads[1].astype(jnp.bfloat16), "col", scatter_dimension=1, tiled=True
        ).astype(jnp.float32),
    )
    return (
        lax.psum_scatter(
            narrowed[0].astype(jnp.bfloat16), "row", scatter_dimension=0, tiled=True
        ).astype(jnp.float32),
        lax.psum_scatter(
            narrowed[1].astype(jnp.bfloat16), "row", scatter_dimension=0, tiled=True
        ).astype(jnp.float32),
    )


def dot_rows(left, right):
    return lax.dot_general(
        left, right, (((0,), (0,)), ((), ())), preferred_element_type=jnp.float32
    )


def dot_back(left, right):
    return lax.dot_general(
        left, right, (((1,), (1,)), ((), ())), preferred_element_type=jnp.float32
    )


def norm_rows(resid, gain, shift):
    centre = resid - jnp.mean(resid, axis=1, keepdims=True)
    factor = lax.rsqrt(jnp.mean(centre * centre, axis=1, keepdims=True) + norm_eps)
    normed = centre * factor
    return (normed * gain + shift, normed, factor)


def norm_back(grad_result, normed, factor, gain):
    grad_normed = grad_result * gain
    grad_resid = factor * (
        grad_normed
        - jnp.mean(grad_normed, axis=1, keepdims=True)
        - normed * jnp.mean(grad_normed * normed, axis=1, keepdims=True)
    )
    return (grad_resid, jnp.sum(grad_result * normed, axis=0), jnp.sum(grad_result, axis=0))


def gelu_exact(value):
    return jax.nn.gelu(value, approximate=False)


def pair_scores(query_part, key_part, seg_query, seg_key):
    query_heads = query_part.reshape(query_part.shape[0], 2, HEAD_DIM)
    key_heads = key_part.reshape(key_part.shape[0], 2, HEAD_DIM)
    raw = jnp.einsum("qhd,khd->hqk", query_heads, key_heads, preferred_element_type=jnp.float32)
    same = seg_query[:, None] == seg_key[None, :]
    return jnp.where(same[None], raw * HEAD_DIM ** (-0.5), masked_score)


def per_device(
    tokens,
    segment,
    w_qkv,
    w_out,
    w_up,
    w_down,
    bias_query,
    bias_value,
    bias_out,
    gain_attn,
    shift_attn,
    bias_up,
    bias_down,
    gain_ffn,
    shift_ffn,
    cotangent,
):
    model = tokens.shape[1]
    tok_rows = tokens.shape[0]
    pairs = HEADS // 2
    width = 2 * HEAD_DIM
    qlen = min(tok_rows, LEN)
    local_seqs = tok_rows // qlen
    item_count = local_seqs * pairs
    device_at = lax.axis_index("row") * lax.axis_size("col") + lax.axis_index("col")
    seq_first = device_at * tok_rows // LEN
    attn_qkv, attn_out = gather_block((w_qkv, w_out))
    ffn_up, ffn_down = gather_block((w_up, w_down))
    projected = jnp.dot(tokens, attn_qkv, preferred_element_type=jnp.float32)
    queries = (projected[:, :model] + bias_query).astype(jnp.bfloat16)
    keys_values = jnp.concatenate(
        [projected[:, model : 2 * model], projected[:, 2 * model :] + bias_value], axis=1
    ).astype(jnp.bfloat16)

    def item_place(item):
        seq_at = item // pairs
        pair_at = item % pairs
        return (seq_at, seq_at * qlen, seq_at * LEN, pair_at * width)

    def item_segments(seq_at):
        segrow = lax.dynamic_index_in_dim(segment, seq_first + seq_at, 0, keepdims=False)
        return (segrow, segrow)

    def attend_step(item, carried):
        context, logsum = carried
        seq_at, query_row, key_row, start_col = item_place(item)
        query_part = lax.dynamic_slice(queries, (query_row, start_col), (qlen, width))
        key_part = lax.dynamic_slice(keys_values, (key_row, start_col), (LEN, width))
        value_part = lax.dynamic_slice(keys_values, (key_row, model + start_col), (LEN, width))
        seg_query, seg_key = item_segments(seq_at)
        scores = pair_scores(query_part, key_part, seg_query, seg_key)
        peak = jnp.max(scores, axis=2, keepdims=True)
        expo = jnp.exp(scores - peak)
        total = jnp.sum(expo, axis=2, keepdims=True)
        prob = (expo / total).astype(jnp.bfloat16)
        result = jnp.einsum(
            "hqk,khd->qhd",
            prob,
            value_part.reshape(LEN, 2, HEAD_DIM),
            preferred_element_type=jnp.float32,
        )
        context = lax.dynamic_update_slice(
            context, result.reshape(qlen, width).astype(jnp.bfloat16), (query_row, start_col)
        )
        logsum = lax.dynamic_update_slice(
            logsum, (peak + jnp.log(total))[None, :, :, 0], (item, 0, 0)
        )
        return (context, logsum)

    context, logsum = lax.fori_loop(
        0,
        item_count,
        attend_step,
        (jnp.zeros((tok_rows, model), jnp.bfloat16), jnp.zeros((item_count, 2, qlen), jnp.float32)),
    )
    attended = jnp.dot(context, attn_out, preferred_element_type=jnp.float32) + bias_out
    hidden, normed_one, factor_one = norm_rows(
        tokens.astype(jnp.float32) + attended, gain_attn, shift_attn
    )
    hidden_low = hidden.astype(jnp.bfloat16)
    upward = jnp.dot(hidden_low, ffn_up, preferred_element_type=jnp.float32) + bias_up
    active_low = gelu_exact(upward).astype(jnp.bfloat16)
    ffn_result = jnp.dot(active_low, ffn_down, preferred_element_type=jnp.float32) + bias_down
    output, normed_two, factor_two = norm_rows(hidden + ffn_result, gain_ffn, shift_ffn)
    grad_two, grad_gain_ffn, grad_shift_ffn = norm_back(
        cotangent.astype(jnp.float32), normed_two, factor_two, gain_ffn
    )
    grad_bias_down = jnp.sum(grad_two, axis=0)
    grad_two_low = grad_two.astype(jnp.bfloat16)
    grad_down_full = dot_rows(active_low, grad_two_low)
    grad_active = dot_back(grad_two_low, ffn_down)
    grad_upward = jax.vjp(gelu_exact, upward)[1](grad_active)[0]
    grad_bias_up = jnp.sum(grad_upward, axis=0)
    grad_up_low = grad_upward.astype(jnp.bfloat16)
    grad_up_full = dot_rows(hidden_low, grad_up_low)
    grad_hidden = grad_two + dot_back(grad_up_low, ffn_up)
    block_up, block_down = reduce_grads((grad_up_full, grad_down_full))
    grad_one, grad_gain_attn, grad_shift_attn = norm_back(
        grad_hidden, normed_one, factor_one, gain_attn
    )
    grad_bias_out = jnp.sum(grad_one, axis=0)
    grad_one_low = grad_one.astype(jnp.bfloat16)
    grad_out_full = dot_rows(context, grad_one_low)
    grad_context = dot_back(grad_one_low, attn_out).astype(jnp.bfloat16)

    def back_step(item, carried):
        grad_queries, grad_kv = carried
        seq_at, query_row, key_row, start_col = item_place(item)
        query_part = lax.dynamic_slice(queries, (query_row, start_col), (qlen, width))
        key_part = lax.dynamic_slice(keys_values, (key_row, start_col), (LEN, width))
        value_part = lax.dynamic_slice(keys_values, (key_row, model + start_col), (LEN, width))
        grad_part = lax.dynamic_slice(grad_context, (query_row, start_col), (qlen, width))
        seg_query, seg_key = item_segments(seq_at)
        lse_now = lax.dynamic_index_in_dim(logsum, item, 0, keepdims=False)
        scores = pair_scores(query_part, key_part, seg_query, seg_key)
        prob = jnp.exp(scores - lse_now[:, :, None])
        grad_heads = grad_part.reshape(qlen, 2, HEAD_DIM)
        value_heads = value_part.reshape(LEN, 2, HEAD_DIM)
        grad_prob = jnp.einsum(
            "qhd,khd->hqk", grad_heads, value_heads, preferred_element_type=jnp.float32
        )
        grad_value = jnp.einsum(
            "hqk,qhd->khd",
            prob.astype(jnp.bfloat16),
            grad_heads,
            preferred_element_type=jnp.float32,
        )
        inner = jnp.sum(prob * grad_prob, axis=2, keepdims=True)
        grad_raw = (prob * (grad_prob - inner) * HEAD_DIM ** (-0.5)).astype(jnp.bfloat16)
        grad_query = jnp.einsum(
            "hqk,khd->qhd",
            grad_raw,
            key_part.reshape(LEN, 2, HEAD_DIM),
            preferred_element_type=jnp.float32,
        )
        grad_key = jnp.einsum(
            "hqk,qhd->khd",
            grad_raw,
            query_part.reshape(qlen, 2, HEAD_DIM),
            preferred_element_type=jnp.float32,
        )
        grad_queries = lax.dynamic_update_slice(
            grad_queries, grad_query.reshape(qlen, width), (query_row, start_col)
        )
        grad_kv = lax.dynamic_update_slice(
            grad_kv, grad_key.reshape(LEN, width), (key_row, start_col)
        )
        grad_kv = lax.dynamic_update_slice(
            grad_kv, grad_value.reshape(LEN, width), (key_row, model + start_col)
        )
        return (grad_queries, grad_kv)

    grad_queries, grad_kv_whole = lax.fori_loop(
        0,
        item_count,
        back_step,
        (
            jnp.zeros((tok_rows, model), jnp.float32),
            jnp.zeros((keys_values.shape[0], 2 * model), jnp.float32),
        ),
    )
    grad_kv = grad_kv_whole
    grad_bias_query = jnp.sum(grad_queries, axis=0)
    grad_bias_value = jnp.sum(grad_kv[:, model:], axis=0)
    grad_proj_low = jnp.concatenate([grad_queries, grad_kv], axis=1).astype(jnp.bfloat16)
    grad_qkv_full = dot_rows(tokens, grad_proj_low)
    grad_tokens = grad_one + dot_back(grad_proj_low, attn_qkv)
    block_qkv, block_out = reduce_grads((grad_qkv_full, grad_out_full))
    (
        sum_query,
        sum_value,
        sum_out,
        sum_gain_attn,
        sum_shift_attn,
        sum_up,
        sum_down,
        sum_gain_ffn,
        sum_shift_ffn,
    ) = lax.psum(
        (
            grad_bias_query,
            grad_bias_value,
            grad_bias_out,
            grad_gain_attn,
            grad_shift_attn,
            grad_bias_up,
            grad_bias_down,
            grad_gain_ffn,
            grad_shift_ffn,
        ),
        ("row", "col"),
    )
    return (
        output.astype(jnp.bfloat16),
        grad_tokens,
        block_qkv,
        block_out,
        block_up,
        block_down,
        sum_query,
        sum_value,
        sum_out,
        sum_gain_attn,
        sum_shift_attn,
        sum_up,
        sum_down,
        sum_gain_ffn,
        sum_shift_ffn,
    )


def solution(mesh):
    return jax.shard_map(
        per_device,
        mesh=mesh,
        in_specs=(
            P(("row", "col"), None),
            P(),
            P("row", "col"),
            P("row", "col"),
            P("row", "col"),
            P("row", "col"),
            P(),
            P(),
            P(),
            P(),
            P(),
            P(),
            P(),
            P(),
            P(),
            P(("row", "col"), None),
        ),
        out_specs=(
            P(("row", "col"), None),
            P(("row", "col"), None),
            P("row", "col"),
            P("row", "col"),
            P("row", "col"),
            P("row", "col"),
            P(),
            P(),
            P(),
            P(),
            P(),
            P(),
            P(),
            P(),
            P(),
        ),
        check_vma=False,
    )
```

profile of v0, /device:TPU:0, one launch (start us, length us, event | category | flops | bytes accessed | tf_op | source)
XLA Modules:
  0.0 1040.2 jit_solution(14863380718797404151)
XLA Ops:
  7.2 17.5 %all-gather = bf16[4,576,96]{1,2,0:T(8,128)(2,1)S(1)} all-gather(bf16[1,576,96]{1,2,0:T(8,128)(2,1)} %bitcast.129), channel_id=1, replica_groups=mesh['row'=8,'col'=4] {'col'}, dimensions={0}, use_global_device_ids=true | all-gather | bytes 552960 | tf_op jit(solution)/shard_map/all_gather | solution.py:15
  42.3 18.1 %all_gather.28 = bf16[96,3072]{1,0:T(8,128)(2,1)} all-gather(bf16[96,768]{1,0:T(8,128)(2,1)} %param.24), channel_id=1, replica_groups=mesh['row'=8,'col'=4] {'col'}, dimensions={1}, use_global_device_ids=true | all-gather | bytes 737280 | tf_op jit(solution)/shard_map/all_gather | solution.py:15
  60.5 15.7 %all_gather.30 = bf16[384,768]{0,1:T(8,128)(2,1)} all-gather(bf16[384,192]{0,1:T(8,128)(2,1)S(1)} %copy-done.12), channel_id=1, replica_groups=mesh['row'=8,'col'=4] {'col'}, dimensions={1}, use_global_device_ids=true | all-gather | bytes 737280 | tf_op jit(solution)/shard_map/all_gather | solution.py:16
  95.2 60.3 %while.34 = (s32[]{:T(128)}, bf16[1024,768]{0,1:T(8,128)(2,1)}, f32[6,2,1024]{2,1,0:T(2,128)S(1)}, bf16[1024,1536]{0,1:T(8,128)(2,1)}, s32[]{:T(128)}, /*index=5...) while((s32[]{:T(128)}, bf16[1024,768]{0,1:T(8,128)(2,1)}, ...), condition=%wide.region_3.4_spmd, body=%wide.region_0.3_spmd.sunk | while | flops 563214336 | bytes 32584120 | solution.py:154
  161.1 38.2 %multiply_convert_fusion.1 = (bf16[1024,3072]{1,0:T(8,128)(2,1)}, f32[1024,3072]{1,0:T(8,128)}, f32[1024,3072]{1,0:T(8,128)}) fusion(f32[3072]{0:T(1024)S(1)} %copy-done.23, bf16[768,3072]{1,0:T(8,128)(2,1)} %all-gather.10.cloned.1.call-done, f32[1024,768]{0,1:T(8,128)S(1)} %get-tuple-element.618, f32[768]{0:T(1024)S(1)} %copy-done.26, ...), kind=kOutput, calls=%fused_computation.55 | convolution fusion | flops 5043388416 | bytes 39348224 | tf_op jit(solution)/shard_map/dot_general | solution.py:165
  211.2 19.2 %fusion.90 = (f32[3072]{0:T(1024)}, bf16[1024,3072]{1,0:T(8,128)(2,1)}) fusion(f32[1024,3072]{1,0:T(8,128)} %get-tuple-element.602, bf16[3072,768]{0,1:T(8,128)(2,1)} %all-gather.12.cloned.1.call-done, f32[1024]{0:T(1024)S(1)} %get-tuple-element.625, f32[1024,768]{0,1:T(8,128)S(1)} %get-tuple-element.621, f32[1024]{0:T(1024)S(1)} %broadcast_multiply_fusion.4, ...), kind=kOutput, calls=%fused_computation.132 | convolution fusion | flops 4889244672 | bytes 40938496 | tf_op jit(solution)/shard_map/dot_general | solution.py:50
  259.6 356.7 %while.35 = (s32[]{:T(128)}, f32[1024,768]{0,1:T(8,128)}, f32[1024,1536]{0,1:T(8,128)}, bf16[1024,1536]{0,1:T(8,128)(2,1)}, s32[]{:T(128)}, /*index=5*/s32[32,10...) while((s32[]{:T(128)}, f32[1024,768]{0,1:T(8,128)}, ...), condition=%wide.region_14.15_spmd, body=%wide.region_12.14_spmd.sunk | while | flops 1397757952 | bytes 74240520 | solution.py:237
  279.9 15.0 %fusion.160 = f32[2,64,1024]{2,1,0:T(8,128)} fusion(bf16[1024,2,64]{0,2,1:T(8,128)(2,1)S(1)} %bitcast.113, f32[2,1024,1024]{1,2,0:T(8,128)} %fusion.157, f32[2,1024,1024]{1,2,0:T(8,128)} %fusion.158, f32[2,1024]{1,0:T(2,128)S(1)} %dynamic-slice_bitcast_fusion.2, pred[1024,1024]{0,1:T(8,128)(4,1)} %broadcast_compare_fusion.5), kind=kOutput, calls=%fused_computation.23.clone.1 | convolution fusion | flops 291507200 | bytes 18620416 | tf_op jit(solution)/shard_map/while/body/eval_jaxpr/hqk,khd->qhd/dot_general | solution.py:214
  294.9 15.2 %fusion.159 = f32[2,64,1024]{2,1,0:T(8,128)} fusion(bf16[1024,2,64]{0,2,1:T(8,128)(2,1)} %bitcast.115, f32[2,1024,1024]{1,2,0:T(8,128)} %fusion.157, f32[2,1024,1024]{1,2,0:T(8,128)} %fusion.158, f32[2,1024]{1,0:T(2,128)S(1)} %dynamic-slice_bitcast_fusion.2, pred[1024,1024]{0,1:T(8,128)(4,1)} %broadcast_compare_fusion.5), kind=kOutput, calls=%fused_computation.22.clone.1 | convolution fusion | flops 291507200 | bytes 18620416 | tf_op jit(solution)/shard_map/while/body/eval_jaxpr/hqk,qhd->khd/dot_general | solution.py:220
  354.2 15.2 %fusion.159 = f32[2,64,1024]{2,1,0:T(8,128)} fusion(bf16[1024,2,64]{0,2,1:T(8,128)(2,1)} %bitcast.115, f32[2,1024,1024]{1,2,0:T(8,128)} %fusion.157, f32[2,1024,1024]{1,2,0:T(8,128)} %fusion.158, f32[2,1024]{1,0:T(2,128)S(1)} %dynamic-slice_bitcast_fusion.2, pred[1024,1024]{0,1:T(8,128)(4,1)} %broadcast_compare_fusion.5), kind=kOutput, calls=%fused_computation.22.clone.1 | convolution fusion | flops 291507200 | bytes 18620416 | tf_op jit(solution)/shard_map/while/body/eval_jaxpr/hqk,qhd->khd/dot_general | solution.py:220
  398.6 15.0 %fusion.160 = f32[2,64,1024]{2,1,0:T(8,128)} fusion(bf16[1024,2,64]{0,2,1:T(8,128)(2,1)S(1)} %bitcast.113, f32[2,1024,1024]{1,2,0:T(8,128)} %fusion.157, f32[2,1024,1024]{1,2,0:T(8,128)} %fusion.158, f32[2,1024]{1,0:T(2,128)S(1)} %dynamic-slice_bitcast_fusion.2, pred[1024,1024]{0,1:T(8,128)(4,1)} %broadcast_compare_fusion.5), kind=kOutput, calls=%fused_computation.23.clone.1 | convolution fusion | flops 291507200 | bytes 18620416 | tf_op jit(solution)/shard_map/while/body/eval_jaxpr/hqk,khd->qhd/dot_general | solution.py:214
  413.6 15.2 %fusion.159 = f32[2,64,1024]{2,1,0:T(8,128)} fusion(bf16[1024,2,64]{0,2,1:T(8,128)(2,1)} %bitcast.115, f32[2,1024,1024]{1,2,0:T(8,128)} %fusion.157, f32[2,1024,1024]{1,2,0:T(8,128)} %fusion.158, f32[2,1024]{1,0:T(2,128)S(1)} %dynamic-slice_bitcast_fusion.2, pred[1024,1024]{0,1:T(8,128)(4,1)} %broadcast_compare_fusion.5), kind=kOutput, calls=%fused_computation.22.clone.1 | convolution fusion | flops 291507200 | bytes 18620416 | tf_op jit(solution)/shard_map/while/body/eval_jaxpr/hqk,qhd->khd/dot_general | solution.py:220
  458.0 15.0 %fusion.160 = f32[2,64,1024]{2,1,0:T(8,128)} fusion(bf16[1024,2,64]{0,2,1:T(8,128)(2,1)S(1)} %bitcast.113, f32[2,1024,1024]{1,2,0:T(8,128)} %fusion.157, f32[2,1024,1024]{1,2,0:T(8,128)} %fusion.158, f32[2,1024]{1,0:T(2,128)S(1)} %dynamic-slice_bitcast_fusion.2, pred[1024,1024]{0,1:T(8,128)(4,1)} %broadcast_compare_fusion.5), kind=kOutput, calls=%fused_computation.23.clone.1 | convolution fusion | flops 291507200 | bytes 18620416 | tf_op jit(solution)/shard_map/while/body/eval_jaxpr/hqk,khd->qhd/dot_general | solution.py:214
  473.0 15.2 %fusion.159 = f32[2,64,1024]{2,1,0:T(8,128)} fusion(bf16[1024,2,64]{0,2,1:T(8,128)(2,1)} %bitcast.115, f32[2,1024,1024]{1,2,0:T(8,128)} %fusion.157, f32[2,1024,1024]{1,2,0:T(8,128)} %fusion.158, f32[2,1024]{1,0:T(2,128)S(1)} %dynamic-slice_bitcast_fusion.2, pred[1024,1024]{0,1:T(8,128)(4,1)} %broadcast_compare_fusion.5), kind=kOutput, calls=%fused_computation.22.clone.1 | convolution fusion | flops 291507200 | bytes 18620416 | tf_op jit(solution)/shard_map/while/body/eval_jaxpr/hqk,qhd->khd/dot_general | solution.py:220
  517.4 15.0 %fusion.160 = f32[2,64,1024]{2,1,0:T(8,128)} fusion(bf16[1024,2,64]{0,2,1:T(8,128)(2,1)S(1)} %bitcast.113, f32[2,1024,1024]{1,2,0:T(8,128)} %fusion.157, f32[2,1024,1024]{1,2,0:T(8,128)} %fusion.158, f32[2,1024]{1,0:T(2,128)S(1)} %dynamic-slice_bitcast_fusion.2, pred[1024,1024]{0,1:T(8,128)(4,1)} %broadcast_compare_fusion.5), kind=kOutput, calls=%fused_computation.23.clone.1 | convolution fusion | flops 291507200 | bytes 18620416 | tf_op jit(solution)/shard_map/while/body/eval_jaxpr/hqk,khd->qhd/dot_general | solution.py:214
  532.4 15.2 %fusion.159 = f32[2,64,1024]{2,1,0:T(8,128)} fusion(bf16[1024,2,64]{0,2,1:T(8,128)(2,1)} %bitcast.115, f32[2,1024,1024]{1,2,0:T(8,128)} %fusion.157, f32[2,1024,1024]{1,2,0:T(8,128)} %fusion.158, f32[2,1024]{1,0:T(2,128)S(1)} %dynamic-slice_bitcast_fusion.2, pred[1024,1024]{0,1:T(8,128)(4,1)} %broadcast_compare_fusion.5), kind=kOutput, calls=%fused_computation.22.clone.1 | convolution fusion | flops 291507200 | bytes 18620416 | tf_op jit(solution)/shard_map/while/body/eval_jaxpr/hqk,qhd->khd/dot_general | solution.py:220
  576.8 15.0 %fusion.160 = f32[2,64,1024]{2,1,0:T(8,128)} fusion(bf16[1024,2,64]{0,2,1:T(8,128)(2,1)S(1)} %bitcast.113, f32[2,1024,1024]{1,2,0:T(8,128)} %fusion.157, f32[2,1024,1024]{1,2,0:T(8,128)} %fusion.158, f32[2,1024]{1,0:T(2,128)S(1)} %dynamic-slice_bitcast_fusion.2, pred[1024,1024]{0,1:T(8,128)(4,1)} %broadcast_compare_fusion.5), kind=kOutput, calls=%fused_computation.23.clone.1 | convolution fusion | flops 291507200 | bytes 18620416 | tf_op jit(solution)/shard_map/while/body/eval_jaxpr/hqk,khd->qhd/dot_general | solution.py:214
  591.7 15.2 %fusion.159 = f32[2,64,1024]{2,1,0:T(8,128)} fusion(bf16[1024,2,64]{0,2,1:T(8,128)(2,1)} %bitcast.115, f32[2,1024,1024]{1,2,0:T(8,128)} %fusion.157, f32[2,1024,1024]{1,2,0:T(8,128)} %fusion.158, f32[2,1024]{1,0:T(2,128)S(1)} %dynamic-slice_bitcast_fusion.2, pred[1024,1024]{0,1:T(8,128)(4,1)} %broadcast_compare_fusion.5), kind=kOutput, calls=%fused_computation.22.clone.1 | convolution fusion | flops 291507200 | bytes 18620416 | tf_op jit(solution)/shard_map/while/body/eval_jaxpr/hqk,qhd->khd/dot_general | solution.py:220
  651.3 46.1 %reduce-scatter.15.cloned.1.call-done = bf16[768,576]{0,1:T(8,128)(2,1)} async-done(((bf16[768,2304]{0,1:T(8,128)(2,1)}), bf16[768,576]{0,1:T(8,128)(2,1)}) %reduce-scatter.15.cloned.1.call-update) | async-done | bytes 884752 | tf_op jit(solution)/shard_map/reduce_scatter | solution.py:26
  699.6 85.5 %reduce-scatter.23.cloned.1.call-done = bf16[3072,192]{0,1:T(8,128)(2,1)} async-done(((bf16[3072,768]{0,1:T(8,128)(2,1)}), bf16[3072,192]{0,1:T(8,128)(2,1)}) %reduce-scatter.23.cloned.1.call-update) | async-done | bytes 1179664 | tf_op jit(solution)/shard_map/reduce_scatter | solution.py:29
  787.7 85.6 %reduce-scatter.19.cloned.1.call-done = bf16[768,768]{1,0:T(8,128)(2,1)} async-done(((bf16[768,3072]{1,0:T(8,128)(2,1)}), bf16[768,768]{1,0:T(8,128)(2,1)}) %reduce-scatter.19.cloned.1.call-update) | async-done | bytes 1179664 | tf_op jit(solution)/shard_map/reduce_scatter | solution.py:26
  895.8 42.1 %all-reduce = (f32[768]{0:T(1024)}, f32[768]{0:T(1024)}, f32[768]{0:T(1024)}, f32[768]{0:T(1024)}, f32[768]{0:T(1024)}, /*index=5*/f32[3072]{0:T(1024)}, f32[768]{0:T(1024)}, f32[768]{0:T(1024)}, f32[768]{0:T(1024)}) all-reduce(f32[768]{0:T(1024)S(1)} %get-tuple-element.615, ...), channel_id=1, replica_groups=mesh['row'=8,'col'=4] {'row','col'}, use_global_device_ids=true, to_apply=%region_24.25 | all-reduce | flops 9216 | bytes 73728 | tf_op jit(solution)/shard_map/psum | solution.py:263
  951.6 39.7 %reduce-scatter.29.cloned.1.call-done = bf16[384,192]{1,0:T(8,128)(2,1)} async-done(((bf16[3072,192]{1,0:T(8,128)(2,1)}), bf16[384,192]{1,0:T(8,128)(2,1)}) %reduce-scatter.29.cloned.1.call-update) | async-done | bytes 147472
  993.2 38.0 %reduce-scatter.21.cloned.1.call-done = bf16[96,768]{1,0:T(8,128)(2,1)} async-done(((bf16[768,768]{1,0:T(8,128)(2,1)}), bf16[96,768]{1,0:T(8,128)(2,1)}) %reduce-scatter.21.cloned.1.call-update) | async-done | bytes 147472 | tf_op jit(solution)/shard_map/reduce_scatter | solution.py:34
  (281 shorter events, 412.3 us)
Async XLA Ops:
  7.2 53.3 %copy-start.12 = (bf16[384,192]{0,1:T(8,128)(2,1)S(1)}, bf16[384,192]{0,1:T(8,128)(2,1)}, u32[]{:S(2)}) copy-start(bf16[384,192]{0,1:T(8,128)(2,1)} %param.25) | copy-start | bytes 442372
  7.2 73.3 %all-gather.6.cloned.1.call-start = ((), (), s32[]{:S(2)}) async-start(), calls=%async_computation.8 | async-start | bytes 3981312 | tf_op jit(solution)/shard_map/all_gather | solution.py:19
  24.9 54.0 %copy-start.9 = (bf16[1024,768]{1,0:T(8,128)(2,1)S(1)}, bf16[1024,768]{1,0:T(8,128)(2,1)}, u32[]{:S(2)}) copy-start(bf16[1024,768]{1,0:T(8,128)(2,1)} %param.35) | copy-start | bytes 4718596
  26.2 129.4 %all-gather.8.cloned.1.call-start = ((), (), s32[]{:S(2)}) async-start(), calls=%async_computation.9 | async-start | bytes 1327104 | tf_op jit(solution)/shard_map/all_gather | solution.py:20
  42.2 118.9 %all-gather.10.cloned.1.call-start = ((), (), s32[]{:S(2)}) async-start(), calls=%async_computation.10 | async-start | bytes 5308416 | tf_op jit(solution)/shard_map/all_gather | solution.py:19
  60.4 138.9 %all-gather.12.cloned.1.call-start = ((), (), s32[]{:S(2)}) async-start(), calls=%async_computation.11 | async-start | bytes 5308416 | tf_op jit(solution)/shard_map/all_gather | solution.py:20
  76.2 573.0 %reduce-scatter.17.cloned.1.call-start = ((), (), s32[]{:S(2)}) async-start(), calls=%async_computation.13 | async-start | bytes 1474560 | tf_op jit(solution)/shard_map/reduce_scatter | solution.py:29
  95.2 61.6 %copy-start.24 = (f32[768]{0:T(1024)S(1)}, f32[768]{0:T(1024)}, u32[]{:S(2)}) copy-start(f32[768]{0:T(1024)} %param.28) | copy-start | bytes 9220
  160.6 38.7 %copy-start.3 = (f32[1024,768]{0,1:T(8,128)}, f32[1024,768]{0,1:T(8,128)S(1)}, u32[]{:S(2)}) copy-start(f32[1024,768]{0,1:T(8,128)S(1)} %get-tuple-element.618) | copy-start | bytes 9437188
  161.0 38.3 %copy-start.25 = (f32[768]{0:T(1024)S(1)}, f32[768]{0:T(1024)}, u32[]{:S(2)}) copy-start(f32[768]{0:T(1024)} %param.32) | copy-start | bytes 9220
  230.4 11.6 %copy-start.4 = (f32[1024,768]{0,1:T(8,128)S(1)}, f32[1024,768]{0,1:T(8,128)}, u32[]{:S(2)}) copy-start(f32[1024,768]{0,1:T(8,128)} %copy-done.3) | copy-start | bytes 9437188
  249.2 448.1 %reduce-scatter.15.cloned.1.call-start = ((), (), s32[]{:S(2)}) async-start(), calls=%async_computation.12 | async-start | bytes 4423680 | tf_op jit(solution)/shard_map/reduce_scatter | solution.py:26
  294.9 17.5 %copy-start.1 = (bf16[1024,128]{0,1:T(8,128)(2,1)S(1)}, bf16[1024,128]{0,1:T(8,128)(2,1)}, u32[]{:S(2)}) copy-start(bf16[1024,128]{0,1:T(8,128)(2,1)} %copy.124) | copy-start | bytes 786436 | tf_op jit(solution)/shard_map/while
  354.2 17.5 %copy-start.1 = (bf16[1024,128]{0,1:T(8,128)(2,1)S(1)}, bf16[1024,128]{0,1:T(8,128)(2,1)}, u32[]{:S(2)}) copy-start(bf16[1024,128]{0,1:T(8,128)(2,1)} %copy.124) | copy-start | bytes 786436 | tf_op jit(solution)/shard_map/while
  413.6 17.5 %copy-start.1 = (bf16[1024,128]{0,1:T(8,128)(2,1)S(1)}, bf16[1024,128]{0,1:T(8,128)(2,1)}, u32[]{:S(2)}) copy-start(bf16[1024,128]{0,1:T(8,128)(2,1)} %copy.124) | copy-start | bytes 786436 | tf_op jit(solution)/shard_map/while
  473.0 17.5 %copy-start.1 = (bf16[1024,128]{0,1:T(8,128)(2,1)S(1)}, bf16[1024,128]{0,1:T(8,128)(2,1)}, u32[]{:S(2)}) copy-start(bf16[1024,128]{0,1:T(8,128)(2,1)} %copy.124) | copy-start | bytes 786436 | tf_op jit(solution)/shard_map/while
  532.4 17.5 %copy-start.1 = (bf16[1024,128]{0,1:T(8,128)(2,1)S(1)}, bf16[1024,128]{0,1:T(8,128)(2,1)}, u32[]{:S(2)}) copy-start(bf16[1024,128]{0,1:T(8,128)(2,1)} %copy.124) | copy-start | bytes 786436 | tf_op jit(solution)/shard_map/while
  591.7 17.5 %copy-start.1 = (bf16[1024,128]{0,1:T(8,128)(2,1)S(1)}, bf16[1024,128]{0,1:T(8,128)(2,1)}, u32[]{:S(2)}) copy-start(bf16[1024,128]{0,1:T(8,128)(2,1)} %copy.124) | copy-start | bytes 786436 | tf_op jit(solution)/shard_map/while
  629.0 156.1 %reduce-scatter.23.cloned.1.call-start = ((), (), s32[]{:S(2)}) async-start(), calls=%async_computation.16 | async-start | bytes 5898240 | tf_op jit(solution)/shard_map/reduce_scatter | solution.py:29
  638.7 234.5 %reduce-scatter.19.cloned.1.call-start = ((), (), s32[]{:S(2)}) async-start(), calls=%async_computation.14 | async-start | bytes 5898240 | tf_op jit(solution)/shard_map/reduce_scatter | solution.py:26
  649.2 288.7 %reduce-scatter.27.cloned.1.call-start = ((), (), s32[]{:S(2)}) async-start(), calls=%async_computation.18 | async-start | bytes 442368
  651.2 298.5 %reduce-scatter.25.cloned.1.call-start = ((), (), s32[]{:S(2)}) async-start(), calls=%async_computation.17 | async-start | bytes 1105920
  699.6 291.8 %reduce-scatter.29.cloned.1.call-start = ((), (), s32[]{:S(2)}) async-start(), calls=%async_computation.19 | async-start | bytes 1769472
  787.6 243.5 %reduce-scatter.21.cloned.1.call-start = ((), (), s32[]{:S(2)}) async-start(), calls=%async_computation.15 | async-start | bytes 1327104 | tf_op jit(solution)/shard_map/reduce_scatter | solution.py:34
  (26 other events, 83.2 us)
Sparse Core Ops, SparseCore 0:
  26.3 35.5 all-gather.5
  64.4 23.9 all-gather.7
  90.2 38.7 all-gather.9
  130.7 39.6 all-gather.11
  249.4 30.9 reduce-scatter.16
  629.1 68.1 reduce-scatter.14
  699.6 85.4 reduce-scatter.22
  787.4 85.7 reduce-scatter.18
  876.3 34.3 reduce-scatter.26
  913.8 35.9 reduce-scatter.24
  953.0 38.2 reduce-scatter.28
  994.5 36.6 reduce-scatter.20
where the time goes:
time: 1050 us; the launch traced here: 1040 us
  matrix products  439 us (42%)
  waiting for transfers between devices  305 us (29%)
  local copies, waits for them, and re-layouts  128 us (12%)
  blocking collectives  108 us (10%)
  other arithmetic  43.5 us (4%)
  between operations  15.1 us (1%)
    reduce_scatter x2, waiting for transfers between devices, reduce_grads(): lax.psum_scatter(grads[0].astype(jnp.bfloat16), 'col', scatter_dimension=...  132 us
    dot_general x6, matrix products, back_step(): jnp.einsum('hqk,qhd->khd', grad_raw, query_part.reshape(qlen, 2, HEAD_DIM...  91.2 us
    dot_general x6, matrix products, back_step(): jnp.einsum('hqk,khd->qhd', grad_raw, key_part.reshape(LEN, 2, HEAD_DIM),...  89.8 us
    reduce_scatter x2, waiting for transfers between devices, reduce_grads(): lax.psum_scatter(grads[1].astype(jnp.bfloat16), 'col', scatter_dimension=...  85.5 us
    unnamed x15, waiting for transfers between devices  50.1 us
    dot_general x4, matrix products, dot_back(): lax.dot_general(left, right, (((1,), (1,)), ((), ())), preferred_element_...  45.4 us
    psum x1, blocking collectives, per_device(): lax.psum((grad_bias_query, grad_bias_value, grad_bias_out, grad_gain_attn...  42.1 us
    dot_general x12, matrix products, pair_scores(): jnp.einsum('qhd,khd->hqk', query_heads, key_heads, preferred_element_type...  38.5 us
  transfers between devices with their start and end apart: 12, of which 6 were waited for; matrix products, arithmetic and copies ran while one was open for 53% of the time, Pallas kernels for 0%

commit v1 on v0

--- a/solution.py
+++ b/solution.py
@@ -2,6 +2,7 @@
 import jax.numpy as jnp
 from jax import lax
 from jax.sharding import PartitionSpec as P
+from jax.lax import axis_index, axis_size, ppermute
 
 HEADS = 12
 HEAD_DIM = 64
@@ -10,10 +11,38 @@
 masked_score = -1e30
 
 
+def work_signs_over_axis(v0, axis_k):
+    outer = list(v0.shape[1:])
+    outer[axis_k] *= v0.shape[0]
+    aux = jnp.moveaxis(v0, 0, axis_k).reshape(outer)
+    return aux
+
+
+def review_waves_on_mesh(chunk, comm_axis):
+    carry_out, d_next = (axis_size(comm_axis), axis_index(comm_axis))
+    h_now, part_now = (chunk[None], 1)
+    while part_now < carry_out:
+        queue = []
+        no = 0
+        while no < carry_out:
+            queue.append((no, no ^ part_now))
+            no += 1
+        prior = ppermute(h_now, comm_axis, queue)
+        heard = d_next & part_now == 0
+        h_now = jnp.concatenate([jnp.where(heard, h_now, prior), jnp.where(heard, prior, h_now)])
+        part_now *= 2
+    return h_now
+
+
 def gather_block(blocks):
+
+    def report_the_orders(inner_x, x_part, dim_k):
+        opened = work_signs_over_axis(review_waves_on_mesh(inner_x, x_part), dim_k)
+        return opened
+
     widened = (
         lax.all_gather(blocks[0], "col", axis=1, tiled=True),
-        lax.all_gather(blocks[1], "col", axis=1, tiled=True),
+        report_the_orders(blocks[1], "col", 1),
     )
     return (
         lax.all_gather(widened[0], "row", axis=0, tiled=True),

time: 1050 us -> 1040 us (level)
  blocking collectives: 108 us -> 78.6 us
  waiting for transfers between devices: 305 us -> 322 us
    all_gather x2 -> x0, blocking collectives: 30 us -> none  [gather_block(): lax.all_gather(blocks[1], 'col', axis=1, tiled=True)]
    ppermute x0 -> x4, waiting for transfers between devices: none -> 19.2 us  [review_waves_on_mesh(): prior = ppermute(h_now, comm_axis, queue)]
    unnamed x66 -> x67, local copies, waits for them, and re-layouts: 30.7 us -> 28.8 us
  transfers between devices with their start and end apart: 12 -> 16, of which waited for: 6 -> 10; matrix products, arithmetic and copies ran while one was open for 53% -> 53% of each run, Pallas kernels for 0% -> 0%
where the time goes in v1:
time: 1040 us
  matrix products  439 us (42%)
  waiting for transfers between devices  322 us (31%)
  local copies, waits for them, and re-layouts  126 us (12%)
  blocking collectives  78.6 us (8%)
  other arithmetic  49 us (5%)
  between operations  15.1 us (1%)
    reduce_scatter x2, waiting for transfers between devices, reduce_grads(): lax.psum_scatter(grads[0].astype(jnp.bfloat16), 'col', scatter_dimension=...  129 us
    dot_general x6, matrix products, back_step(): jnp.einsum('hqk,qhd->khd', grad_raw, query_part.reshape(qlen, 2, HEAD_DIM...  91 us
    dot_general x6, matrix products, back_step(): jnp.einsum('hqk,khd->qhd', grad_raw, key_part.reshape(LEN, 2, HEAD_DIM),...  89.8 us
    reduce_scatter x2, waiting for transfers between devices, reduce_grads(): lax.psum_scatter(grads[1].astype(jnp.bfloat16), 'col', scatter_dimension=...  85.5 us
    unnamed x15, waiting for transfers between devices  50.1 us
    dot_general x4, matrix products, dot_back(): lax.dot_general(left, right, (((1,), (1,)), ((), ())), preferred_element_...  45.4 us
    psum x1, blocking collectives, per_device(): lax.psum((grad_bias_query, grad_bias_value, grad_bias_out, grad_gain_attn...  42.1 us
    dot_general x12, matrix products, pair_scores(): jnp.einsum('qhd,khd->hqk', query_heads, key_heads, preferred_element_type...  38.4 us
  transfers between devices with their start and end apart: 16, of which 10 were waited for; matrix products, arithmetic and copies ran while one was open for 53% of the time, Pallas kernels for 0%

profile of v1, /device:TPU:0, one launch (start us, length us, event | category | flops | bytes accessed | tf_op | source)
XLA Modules:
  0.0 1037.9 jit_solution(4045979018817789024)
XLA Ops:
  7.2 17.5 %all-gather = bf16[4,576,96]{1,2,0:T(8,128)(2,1)S(1)} all-gather(bf16[1,576,96]{1,2,0:T(8,128)(2,1)} %bitcast.142), channel_id=1, replica_groups=mesh['row'=8,'col'=4] {'col'}, dimensions={0}, use_global_device_ids=true | all-gather | bytes 552960 | tf_op jit(solution)/shard_map/all_gather | solution.py:44
  39.5 19.1 %all_gather.21 = bf16[96,3072]{1,0:T(8,128)(2,1)} all-gather(bf16[96,768]{1,0:T(8,128)(2,1)S(1)} %copy-done.13), channel_id=1, replica_groups=mesh['row'=8,'col'=4] {'col'}, dimensions={1}, use_global_device_ids=true | all-gather | bytes 737280 | tf_op jit(solution)/shard_map/all_gather | solution.py:44
  95.3 60.2 %while.34 = (s32[]{:T(128)}, bf16[1024,768]{0,1:T(8,128)(2,1)}, f32[6,2,1024]{2,1,0:T(2,128)S(1)}, bf16[1024,1536]{0,1:T(8,128)(2,1)}, s32[]{:T(128)}, /*index=5...) while((s32[]{:T(128)}, bf16[1024,768]{0,1:T(8,128)(2,1)}, ...), condition=%wide.region_3.4_spmd, body=%wide.region_0.3_spmd.sunk | while | flops 563214336 | bytes 32584120 | solution.py:183
  161.0 38.3 %multiply_convert_fusion.1 = (bf16[1024,3072]{1,0:T(8,128)(2,1)}, f32[1024,3072]{1,0:T(8,128)}, f32[1024,3072]{1,0:T(8,128)}) fusion(f32[3072]{0:T(1024)S(1)} %copy-done.24, bf16[768,3072]{1,0:T(8,128)(2,1)} %all-gather.10.cloned.1.call-done, f32[1024,768]{0,1:T(8,128)S(1)} %get-tuple-element.595, f32[768]{0:T(1024)S(1)} %copy-done.27, ...), kind=kOutput, calls=%fused_computation.55 | convolution fusion | flops 5043388416 | bytes 39348224 | tf_op jit(solution)/shard_map/dot_general | solution.py:194
  211.3 19.2 %fusion.90 = (f32[3072]{0:T(1024)}, bf16[1024,3072]{1,0:T(8,128)(2,1)}) fusion(f32[1024,3072]{1,0:T(8,128)} %get-tuple-element.571, bf16[3072,768]{0,1:T(8,128)(2,1)} %all-gather.12.cloned.1.call-done, f32[1024]{0:T(1024)S(1)} %get-tuple-element.602, f32[1024,768]{0,1:T(8,128)S(1)} %get-tuple-element.598, f32[1024]{0:T(1024)S(1)} %broadcast_multiply_fusion.4, ...), kind=kOutput, calls=%fused_computation.144 | convolution fusion | flops 4889244672 | bytes 40938496 | tf_op jit(solution)/shard_map/dot_general | solution.py:79
  259.7 356.5 %while.35 = (s32[]{:T(128)}, f32[1024,768]{0,1:T(8,128)}, f32[1024,1536]{0,1:T(8,128)}, bf16[1024,1536]{0,1:T(8,128)(2,1)}, s32[]{:T(128)}, /*index=5*/s32[32,10...) while((s32[]{:T(128)}, f32[1024,768]{0,1:T(8,128)}, ...), condition=%wide.region_14.15_spmd, body=%wide.region_12.14_spmd.sunk | while | flops 1397757952 | bytes 74240520 | solution.py:266
  279.9 15.0 %fusion.160 = f32[2,64,1024]{2,1,0:T(8,128)} fusion(bf16[1024,2,64]{0,2,1:T(8,128)(2,1)S(1)} %bitcast.124, f32[2,1024,1024]{1,2,0:T(8,128)} %fusion.157, f32[2,1024,1024]{1,2,0:T(8,128)} %fusion.158, f32[2,1024]{1,0:T(2,128)S(1)} %dynamic-slice_bitcast_fusion.2, pred[1024,1024]{0,1:T(8,128)(4,1)} %broadcast_compare_fusion.5), kind=kOutput, calls=%fused_computation.23.clone.1 | convolution fusion | flops 291507200 | bytes 18620416 | tf_op jit(solution)/shard_map/while/body/eval_jaxpr/hqk,khd->qhd/dot_general | solution.py:243
  294.9 15.2 %fusion.159 = f32[2,64,1024]{2,1,0:T(8,128)} fusion(bf16[1024,2,64]{0,2,1:T(8,128)(2,1)} %bitcast.126, f32[2,1024,1024]{1,2,0:T(8,128)} %fusion.157, f32[2,1024,1024]{1,2,0:T(8,128)} %fusion.158, f32[2,1024]{1,0:T(2,128)S(1)} %dynamic-slice_bitcast_fusion.2, pred[1024,1024]{0,1:T(8,128)(4,1)} %broadcast_compare_fusion.5), kind=kOutput, calls=%fused_computation.22.clone.1 | convolution fusion | flops 291507200 | bytes 18620416 | tf_op jit(solution)/shard_map/while/body/eval_jaxpr/hqk,qhd->khd/dot_general | solution.py:249
  339.3 15.0 %fusion.160 = f32[2,64,1024]{2,1,0:T(8,128)} fusion(bf16[1024,2,64]{0,2,1:T(8,128)(2,1)S(1)} %bitcast.124, f32[2,1024,1024]{1,2,0:T(8,128)} %fusion.157, f32[2,1024,1024]{1,2,0:T(8,128)} %fusion.158, f32[2,1024]{1,0:T(2,128)S(1)} %dynamic-slice_bitcast_fusion.2, pred[1024,1024]{0,1:T(8,128)(4,1)} %broadcast_compare_fusion.5), kind=kOutput, calls=%fused_computation.23.clone.1 | convolution fusion | flops 291507200 | bytes 18620416 | tf_op jit(solution)/shard_map/while/body/eval_jaxpr/hqk,khd->qhd/dot_general | solution.py:243
  354.2 15.2 %fusion.159 = f32[2,64,1024]{2,1,0:T(8,128)} fusion(bf16[1024,2,64]{0,2,1:T(8,128)(2,1)} %bitcast.126, f32[2,1024,1024]{1,2,0:T(8,128)} %fusion.157, f32[2,1024,1024]{1,2,0:T(8,128)} %fusion.158, f32[2,1024]{1,0:T(2,128)S(1)} %dynamic-slice_bitcast_fusion.2, pred[1024,1024]{0,1:T(8,128)(4,1)} %broadcast_compare_fusion.5), kind=kOutput, calls=%fused_computation.22.clone.1 | convolution fusion | flops 291507200 | bytes 18620416 | tf_op jit(solution)/shard_map/while/body/eval_jaxpr/hqk,qhd->khd/dot_general | solution.py:249
  398.6 15.0 %fusion.160 = f32[2,64,1024]{2,1,0:T(8,128)} fusion(bf16[1024,2,64]{0,2,1:T(8,128)(2,1)S(1)} %bitcast.124, f32[2,1024,1024]{1,2,0:T(8,128)} %fusion.157, f32[2,1024,1024]{1,2,0:T(8,128)} %fusion.158, f32[2,1024]{1,0:T(2,128)S(1)} %dynamic-slice_bitcast_fusion.2, pred[1024,1024]{0,1:T(8,128)(4,1)} %broadcast_compare_fusion.5), kind=kOutput, calls=%fused_computation.23.clone.1 | convolution fusion | flops 291507200 | bytes 18620416 | tf_op jit(solution)/shard_map/while/body/eval_jaxpr/hqk,khd->qhd/dot_general | solution.py:243
  413.6 15.2 %fusion.159 = f32[2,64,1024]{2,1,0:T(8,128)} fusion(bf16[1024,2,64]{0,2,1:T(8,128)(2,1)} %bitcast.126, f32[2,1024,1024]{1,2,0:T(8,128)} %fusion.157, f32[2,1024,1024]{1,2,0:T(8,128)} %fusion.158, f32[2,1024]{1,0:T(2,128)S(1)} %dynamic-slice_bitcast_fusion.2, pred[1024,1024]{0,1:T(8,128)(4,1)} %broadcast_compare_fusion.5), kind=kOutput, calls=%fused_computation.22.clone.1 | convolution fusion | flops 291507200 | bytes 18620416 | tf_op jit(solution)/shard_map/while/body/eval_jaxpr/hqk,qhd->khd/dot_general | solution.py:249
  458.0 15.0 %fusion.160 = f32[2,64,1024]{2,1,0:T(8,128)} fusion(bf16[1024,2,64]{0,2,1:T(8,128)(2,1)S(1)} %bitcast.124, f32[2,1024,1024]{1,2,0:T(8,128)} %fusion.157, f32[2,1024,1024]{1,2,0:T(8,128)} %fusion.158, f32[2,1024]{1,0:T(2,128)S(1)} %dynamic-slice_bitcast_fusion.2, pred[1024,1024]{0,1:T(8,128)(4,1)} %broadcast_compare_fusion.5), kind=kOutput, calls=%fused_computation.23.clone.1 | convolution fusion | flops 291507200 | bytes 18620416 | tf_op jit(solution)/shard_map/while/body/eval_jaxpr/hqk,khd->qhd/dot_general | solution.py:243
  472.9 15.2 %fusion.159 = f32[2,64,1024]{2,1,0:T(8,128)} fusion(bf16[1024,2,64]{0,2,1:T(8,128)(2,1)} %bitcast.126, f32[2,1024,1024]{1,2,0:T(8,128)} %fusion.157, f32[2,1024,1024]{1,2,0:T(8,128)} %fusion.158, f32[2,1024]{1,0:T(2,128)S(1)} %dynamic-slice_bitcast_fusion.2, pred[1024,1024]{0,1:T(8,128)(4,1)} %broadcast_compare_fusion.5), kind=kOutput, calls=%fused_computation.22.clone.1 | convolution fusion | flops 291507200 | bytes 18620416 | tf_op jit(solution)/shard_map/while/body/eval_jaxpr/hqk,qhd->khd/dot_general | solution.py:249
  517.3 15.0 %fusion.160 = f32[2,64,1024]{2,1,0:T(8,128)} fusion(bf16[1024,2,64]{0,2,1:T(8,128)(2,1)S(1)} %bitcast.124, f32[2,1024,1024]{1,2,0:T(8,128)} %fusion.157, f32[2,1024,1024]{1,2,0:T(8,128)} %fusion.158, f32[2,1024]{1,0:T(2,128)S(1)} %dynamic-slice_bitcast_fusion.2, pred[1024,1024]{0,1:T(8,128)(4,1)} %broadcast_compare_fusion.5), kind=kOutput, calls=%fused_computation.23.clone.1 | convolution fusion | flops 291507200 | bytes 18620416 | tf_op jit(solution)/shard_map/while/body/eval_jaxpr/hqk,khd->qhd/dot_general | solution.py:243
  532.3 15.2 %fusion.159 = f32[2,64,1024]{2,1,0:T(8,128)} fusion(bf16[1024,2,64]{0,2,1:T(8,128)(2,1)} %bitcast.126, f32[2,1024,1024]{1,2,0:T(8,128)} %fusion.157, f32[2,1024,1024]{1,2,0:T(8,128)} %fusion.158, f32[2,1024]{1,0:T(2,128)S(1)} %dynamic-slice_bitcast_fusion.2, pred[1024,1024]{0,1:T(8,128)(4,1)} %broadcast_compare_fusion.5), kind=kOutput, calls=%fused_computation.22.clone.1 | convolution fusion | flops 291507200 | bytes 18620416 | tf_op jit(solution)/shard_map/while/body/eval_jaxpr/hqk,qhd->khd/dot_general | solution.py:249
  576.7 15.0 %fusion.160 = f32[2,64,1024]{2,1,0:T(8,128)} fusion(bf16[1024,2,64]{0,2,1:T(8,128)(2,1)S(1)} %bitcast.124, f32[2,1024,1024]{1,2,0:T(8,128)} %fusion.157, f32[2,1024,1024]{1,2,0:T(8,128)} %fusion.158, f32[2,1024]{1,0:T(2,128)S(1)} %dynamic-slice_bitcast_fusion.2, pred[1024,1024]{0,1:T(8,128)(4,1)} %broadcast_compare_fusion.5), kind=kOutput, calls=%fused_computation.23.clone.1 | convolution fusion | flops 291507200 | bytes 18620416 | tf_op jit(solution)/shard_map/while/body/eval_jaxpr/hqk,khd->qhd/dot_general | solution.py:243
  591.6 15.2 %fusion.159 = f32[2,64,1024]{2,1,0:T(8,128)} fusion(bf16[1024,2,64]{0,2,1:T(8,128)(2,1)} %bitcast.126, f32[2,1024,1024]{1,2,0:T(8,128)} %fusion.157, f32[2,1024,1024]{1,2,0:T(8,128)} %fusion.158, f32[2,1024]{1,0:T(2,128)S(1)} %dynamic-slice_bitcast_fusion.2, pred[1024,1024]{0,1:T(8,128)(4,1)} %broadcast_compare_fusion.5), kind=kOutput, calls=%fused_computation.22.clone.1 | convolution fusion | flops 291507200 | bytes 18620416 | tf_op jit(solution)/shard_map/while/body/eval_jaxpr/hqk,qhd->khd/dot_general | solution.py:249
  651.1 43.9 %reduce-scatter.15.cloned.1.call-done = bf16[768,576]{0,1:T(8,128)(2,1)} async-done(((bf16[768,2304]{0,1:T(8,128)(2,1)}), bf16[768,576]{0,1:T(8,128)(2,1)}) %reduce-scatter.15.cloned.1.call-update) | async-done | bytes 884752 | tf_op jit(solution)/shard_map/reduce_scatter | solution.py:55
  697.3 85.5 %reduce-scatter.23.cloned.1.call-done = bf16[3072,192]{0,1:T(8,128)(2,1)} async-done(((bf16[3072,768]{0,1:T(8,128)(2,1)}), bf16[3072,192]{0,1:T(8,128)(2,1)}) %reduce-scatter.23.cloned.1.call-update) | async-done | bytes 1179664 | tf_op jit(solution)/shard_map/reduce_scatter | solution.py:58
  785.3 85.6 %reduce-scatter.19.cloned.1.call-done = bf16[768,768]{1,0:T(8,128)(2,1)} async-done(((bf16[768,3072]{1,0:T(8,128)(2,1)}), bf16[768,768]{1,0:T(8,128)(2,1)}) %reduce-scatter.19.cloned.1.call-update) | async-done | bytes 1179664 | tf_op jit(solution)/shard_map/reduce_scatter | solution.py:55
  893.5 42.1 %all-reduce = (f32[768]{0:T(1024)}, f32[768]{0:T(1024)}, f32[768]{0:T(1024)}, f32[768]{0:T(1024)}, f32[768]{0:T(1024)}, /*index=5*/f32[3072]{0:T(1024)}, f32[768]{0:T(1024)}, f32[768]{0:T(1024)}, f32[768]{0:T(1024)}) all-reduce(f32[768]{0:T(1024)S(1)} %get-tuple-element.584, ...), channel_id=1, replica_groups=mesh['row'=8,'col'=4] {'row','col'}, use_global_device_ids=true, to_apply=%region_24.25 | all-reduce | flops 9216 | bytes 73728 | tf_op jit(solution)/shard_map/psum | solution.py:292
  949.3 39.8 %reduce-scatter.29.cloned.1.call-done = bf16[384,192]{1,0:T(8,128)(2,1)} async-done(((bf16[3072,192]{1,0:T(8,128)(2,1)}), bf16[384,192]{1,0:T(8,128)(2,1)}) %reduce-scatter.29.cloned.1.call-update) | async-done | bytes 147472
  990.9 38.0 %reduce-scatter.21.cloned.1.call-done = bf16[96,768]{1,0:T(8,128)(2,1)} async-done(((bf16[768,768]{1,0:T(8,128)(2,1)}), bf16[96,768]{1,0:T(8,128)(2,1)}) %reduce-scatter.21.cloned.1.call-update) | async-done | bytes 147472 | tf_op jit(solution)/shard_map/reduce_scatter | solution.py:63
  (297 shorter events, 412.2 us)
Async XLA Ops:
  7.2 32.3 %copy-start.13 = (bf16[96,768]{1,0:T(8,128)(2,1)S(1)}, bf16[96,768]{1,0:T(8,128)(2,1)}, u32[]{:S(2)}) copy-start(bf16[96,768]{1,0:T(8,128)(2,1)} %param.24) | copy-start | bytes 442372
  7.2 61.7 %copy-start.10 = (bf16[1024,768]{1,0:T(8,128)(2,1)S(1)}, bf16[1024,768]{1,0:T(8,128)(2,1)}, u32[]{:S(2)}) copy-start(bf16[1024,768]{1,0:T(8,128)(2,1)} %param.20) | copy-start | bytes 4718596
  7.2 74.1 %all-gather.6.cloned.1.call-start = ((), (), s32[]{:S(2)}) async-start(), calls=%async_computation.8 | async-start | bytes 3981312 | tf_op jit(solution)/shard_map/all_gather | solution.py:48
  26.1 44.4 %copy-start.9 = (bf16[1024,768]{1,0:T(8,128)(2,1)S(1)}, bf16[1024,768]{1,0:T(8,128)(2,1)}, u32[]{:S(2)}) copy-start(bf16[1024,768]{1,0:T(8,128)(2,1)} %param.35) | copy-start | bytes 4718596
  26.2 129.3 %all-gather.8.cloned.1.call-start = ((), (), s32[]{:S(2)}) async-start(), calls=%async_computation.9 | async-start | bytes 1327104 | tf_op jit(solution)/shard_map/all_gather | solution.py:49
  26.2 4.7 collective-permute-start
  31.7 5.7 collective-permute-start.1
  39.4 121.6 %all-gather.10.cloned.1.call-start = ((), (), s32[]{:S(2)}) async-start(), calls=%async_computation.10 | async-start | bytes 5308416 | tf_op jit(solution)/shard_map/all_gather | solution.py:48
  58.6 140.7 %all-gather.12.cloned.1.call-start = ((), (), s32[]{:S(2)}) async-start(), calls=%async_computation.11 | async-start | bytes 5308416 | tf_op jit(solution)/shard_map/all_gather | solution.py:49
  58.6 8.5 collective-permute-start.2
  68.8 10.2 collective-permute-start.3
  81.0 568.1 %reduce-scatter.17.cloned.1.call-start = ((), (), s32[]{:S(2)}) async-start(), calls=%async_computation.13 | async-start | bytes 1474560 | tf_op jit(solution)/shard_map/reduce_scatter | solution.py:58
  95.3 61.4 %copy-start.25 = (f32[768]{0:T(1024)S(1)}, f32[768]{0:T(1024)}, u32[]{:S(2)}) copy-start(f32[768]{0:T(1024)} %param.28) | copy-start | bytes 9220
  160.5 38.7 %copy-start.3 = (f32[1024,768]{0,1:T(8,128)}, f32[1024,768]{0,1:T(8,128)S(1)}, u32[]{:S(2)}) copy-start(f32[1024,768]{0,1:T(8,128)S(1)} %get-tuple-element.595) | copy-start | bytes 9437188
  160.9 38.3 %copy-start.26 = (f32[768]{0:T(1024)S(1)}, f32[768]{0:T(1024)}, u32[]{:S(2)}) copy-start(f32[768]{0:T(1024)} %param.32) | copy-start | bytes 9220
  249.3 445.7 %reduce-scatter.15.cloned.1.call-start = ((), (), s32[]{:S(2)}) async-start(), calls=%async_computation.12 | async-start | bytes 4423680 | tf_op jit(solution)/shard_map/reduce_scatter | solution.py:55
  354.2 17.5 %copy-start.1 = (bf16[1024,128]{0,1:T(8,128)(2,1)S(1)}, bf16[1024,128]{0,1:T(8,128)(2,1)}, u32[]{:S(2)}) copy-start(bf16[1024,128]{0,1:T(8,128)(2,1)} %copy.104) | copy-start | bytes 786436 | tf_op jit(solution)/shard_map/while
  413.6 17.5 %copy-start.1 = (bf16[1024,128]{0,1:T(8,128)(2,1)S(1)}, bf16[1024,128]{0,1:T(8,128)(2,1)}, u32[]{:S(2)}) copy-start(bf16[1024,128]{0,1:T(8,128)(2,1)} %copy.104) | copy-start | bytes 786436 | tf_op jit(solution)/shard_map/while
  628.8 153.9 %reduce-scatter.23.cloned.1.call-start = ((), (), s32[]{:S(2)}) async-start(), calls=%async_computation.16 | async-start | bytes 5898240 | tf_op jit(solution)/shard_map/reduce_scatter | solution.py:58
  638.5 232.4 %reduce-scatter.19.cloned.1.call-start = ((), (), s32[]{:S(2)}) async-start(), calls=%async_computation.14 | async-start | bytes 5898240 | tf_op jit(solution)/shard_map/reduce_scatter | solution.py:55
  649.1 286.6 %reduce-scatter.27.cloned.1.call-start = ((), (), s32[]{:S(2)}) async-start(), calls=%async_computation.18 | async-start | bytes 442368
  651.1 296.4 %reduce-scatter.25.cloned.1.call-start = ((), (), s32[]{:S(2)}) async-start(), calls=%async_computation.17 | async-start | bytes 1105920
  697.2 291.8 %reduce-scatter.29.cloned.1.call-start = ((), (), s32[]{:S(2)}) async-start(), calls=%async_computation.19 | async-start | bytes 1769472
  785.3 243.6 %reduce-scatter.21.cloned.1.call-start = ((), (), s32[]{:S(2)}) async-start(), calls=%async_computation.15 | async-start | bytes 1327104 | tf_op jit(solution)/shard_map/reduce_scatter | solution.py:63
  (31 other events, 163.9 us)
Sparse Core Ops, SparseCore 0:
  26.3 35.5 all-gather.5
  64.4 23.9 all-gather.7
  90.2 38.8 all-gather.9
  130.8 39.6 all-gather.11
  249.4 28.7 reduce-scatter.16
  629.0 65.9 reduce-scatter.14
  697.3 85.4 reduce-scatter.22
  785.1 85.7 reduce-scatter.18
  874.0 34.3 reduce-scatter.26
  911.5 35.9 reduce-scatter.24
  950.7 38.3 reduce-scatter.28
  992.2 36.6 reduce-scatter.20
